TPU v7x, 512 devices: a whole 4x8x8 slice. The times are simulated.
512 devices in a mesh: segment: 4 (over x), chan: 16 (over y, core), dp: 8 (over z).
Axes of the slice: x: 4, y: 8, z: 8, core: 2. Of those that a mesh axis runs over, the one named last changes fastest.
Arguments:
- grad_top: bfloat16 [8, 1536, 256], P('dp', None, 'chan'), may hold values from -6 to 6
- inputs_one: bfloat16 [4, 8, 1536, 256], P('segment', 'dp', 'chan'), may hold values from -6 to 6
- conv_one: bfloat16 [4, 8, 1536, 256], P('segment', 'dp', 'chan'), may hold values from -130 to 130
- inputs_two: bfloat16 [4, 8, 1536, 256], P('segment', 'dp', 'chan'), may hold values from -6 to 6
- conv_two: bfloat16 [4, 8, 1536, 256], P('segment', 'dp', 'chan'), may hold values from -130 to 130
- proj_weight: bfloat16 [4, 2, 1536, 1536], P('segment', None, 'chan'), may hold values from -0.15625 to 0.15625
- conv_weight: bfloat16 [4, 2, 1536, 432], P('segment', None, 'chan'), may hold values from -0.3125 to 0.3125
- norm_gain: float32 [4, 2, 1536], P('segment', None, 'chan'), may hold values from 0.1 to 1.9
- norm_bias: float32 [4, 2, 1536], P('segment', None, 'chan'), may hold values from -4 to 4
Outputs:
- grad_latent: bfloat16 [4, 8, 1536, 256], P('segment', 'dp', None, 'chan')
- grad_proj: float32 [4, 2, 1536, 1536], P('segment', None, 'chan')
- grad_conv: float32 [4, 2, 1536, 432], P('segment', None, 'chan')
- grad_gain: float32 [4, 2, 1536], P('segment', None, 'chan')
- grad_bias: float32 [4, 2, 1536], P('segment', None, 'chan')
All inputs are finite; a program needn't handle non-finite values.
Results may differ from a plain program's by a relative error of at most 0.009.
Values may be sent and summed in bfloat16 or wider, within the bound.
No kernel may reach another device: no remote copies, remote signals or barrier semaphores. Data moves between devices by JAX's collectives and lax.ppermute only.
A program may use at most 64 MiB of HBM per device.

v0:
```python
import jax
import jax.numpy as jnp
from jax import lax
from jax.sharding import PartitionSpec as P

GS = 48
WW = 64
NORM_EPS = 1e-05


def passed_along(block, axis, distance):
    devices = range(lax.axis_size(axis))
    route = [(i - distance, i) for i in devices if i - distance in devices]
    return lax.ppermute(block, axis, route)


def shifted_cells(values, step_row, step_col, img_width):
    length = values.shape[2]
    margin = img_width + 1
    padded = jnp.pad(values, ((0, 0), (0, 0), (margin, margin)))
    start_at = margin + step_row * img_width + step_col
    part_view = lax.slice_in_dim(padded, start_at, start_at + length, axis=2)
    column = jnp.arange(length, dtype=jnp.int32) % img_width
    inside = (column + step_col >= 0) & (column + step_col < img_width)
    return jnp.where(inside, part_view, jnp.zeros((), values.dtype))


def norm_forward(saved_pre, gain_vec, bias_vec):
    chans, positions = saved_pre.shape
    groups_here = chans // GS
    pre = saved_pre.astype(jnp.float32).reshape(groups_here, GS, positions)
    centre = jnp.mean(pre, axis=(1, 2), keepdims=True)
    varied = jnp.mean(jnp.square(pre - centre), axis=(1, 2), keepdims=True)
    inv_std = lax.rsqrt(varied + NORM_EPS)
    normed = (pre - centre) * inv_std
    gain_grid = gain_vec.reshape(groups_here, GS, 1)
    scaled = normed * gain_grid + bias_vec.reshape(groups_here, GS, 1)
    gate_vals = jax.nn.sigmoid(scaled)
    act_bf = (scaled * gate_vals).astype(jnp.bfloat16).reshape(chans, positions)
    return (normed, scaled, gate_vals, inv_std, gain_grid, act_bf)


def conv_backward(grad_act, norm_state, saved_in, w_conv):
    normed, scaled, gate_vals, inv_std, gain_grid, act_bf = norm_state
    groups_here, _, positions = normed.shape
    chans = groups_here * GS
    grad_act = grad_act.reshape(groups_here, GS, positions)
    grad_norm = grad_act * (gate_vals * (1.0 + scaled * (1.0 - gate_vals)))
    gain_grad = jnp.sum(grad_norm * normed, axis=2).reshape(chans)
    bias_grad = jnp.sum(grad_norm, axis=2).reshape(chans)
    weighted = grad_norm * gain_grid
    first_mean = jnp.mean(weighted, axis=(1, 2), keepdims=True)
    second_mean = jnp.mean(weighted * normed, axis=(1, 2), keepdims=True)
    grad_pre = (inv_std * (weighted - first_mean - normed * second_mean)).astype(jnp.bfloat16)
    saved_grid = saved_in.reshape(groups_here, GS, positions)
    taps_w = w_conv.reshape(groups_here, GS, 9, GS)
    conv_parts = []
    back_sum = jnp.zeros((groups_here, GS, positions), jnp.float32)
    for tap_row in (-1, 0, 1):
        for tap_col in (-1, 0, 1):
            tap_at = 3 * (tap_row + 1) + tap_col + 1
            source = shifted_cells(saved_grid, tap_row, tap_col, WW)
            conv_parts.append(
                jnp.einsum("gop,gjp->goj", grad_pre, source, preferred_element_type=jnp.float32)
            )
            spread_back = jnp.einsum(
                "goj,gop->gjp",
                taps_w[:, :, tap_at, :],
                grad_pre,
                preferred_element_type=jnp.float32,
            )
            back_sum = back_sum + shifted_cells(spread_back, -tap_row, -tap_col, WW)
    conv_grad = jnp.stack(conv_parts, axis=2).reshape(chans, 9 * GS)
    branch = back_sum.reshape(chans, positions).astype(jnp.bfloat16)
    return (branch, conv_grad, gain_grad, bias_grad)


def block_sharded(grad_slab, saved_in, saved_pre, w_proj, w_conv, gain_vec, bias_vec):
    norm_state = norm_forward(saved_pre, gain_vec, bias_vec)
    act_bf = norm_state[5]
    grad_piece = lax.all_gather(grad_slab, "chan", axis=1, tiled=True)
    fresh = jnp.dot(w_proj, grad_piece, preferred_element_type=jnp.float32)
    weight_acc = lax.dot_general(
        act_bf, grad_piece, (((1,), (1,)), ((), ())), preferred_element_type=jnp.float32
    )
    branch, conv_grad, gain_grad, bias_grad = conv_backward(fresh, norm_state, saved_in, w_conv)
    returned = lax.all_to_all(branch, "chan", split_axis=1, concat_axis=0, tiled=True)
    out_slab = (grad_slab.astype(jnp.float32) + returned.astype(jnp.float32)).astype(jnp.bfloat16)
    return (out_slab, (weight_acc, conv_grad, gain_grad, bias_grad))


def take_micro(saved_all, index_at):
    return lax.dynamic_index_in_dim(saved_all[0], index_at, 0, keepdims=False)


def per_device(
    grad_top,
    inputs_one,
    conv_one,
    inputs_two,
    conv_two,
    proj_weight,
    conv_weight,
    norm_gain,
    norm_bias,
):
    segments = lax.axis_size("segment")
    segment_at = lax.axis_index("segment")
    local_mb = grad_top.shape[0]
    chans = conv_one.shape[2]
    width_all = proj_weight.shape[3]
    ticks = local_mb + segments - 1
    initial = (
        jnp.zeros(grad_top.shape[1:], jnp.bfloat16),
        jnp.zeros((1,) + grad_top.shape, jnp.bfloat16),
        jnp.zeros((2, chans, width_all), jnp.float32),
        jnp.zeros((2, chans, 9 * GS), jnp.float32),
        jnp.zeros((2, chans), jnp.float32),
        jnp.zeros((2, chans), jnp.float32),
    )

    def one_tick(tick_at, running):
        received, latent, proj_acc, conv_acc, gain_acc, bias_acc = running
        micro_at = tick_at - (segments - 1 - segment_at)
        is_valid = (micro_at >= 0) & (micro_at < local_mb)
        safe_mb = jnp.clip(micro_at, 0, local_mb - 1)
        top_grad = lax.dynamic_index_in_dim(grad_top, safe_mb, 0, keepdims=False)
        entering = jnp.where(segment_at == segments - 1, top_grad, received)
        mid_grad, grads_two = block_sharded(
            entering,
            take_micro(inputs_two, safe_mb),
            take_micro(conv_two, safe_mb),
            proj_weight[0, 1],
            conv_weight[0, 1],
            norm_gain[0, 1],
            norm_bias[0, 1],
        )
        out_grad, grads_one = block_sharded(
            mid_grad,
            take_micro(inputs_one, safe_mb),
            take_micro(conv_one, safe_mb),
            proj_weight[0, 0],
            conv_weight[0, 0],
            norm_gain[0, 0],
            norm_bias[0, 0],
        )
        weight_mask = is_valid.astype(jnp.float32)
        proj_acc = proj_acc + weight_mask * jnp.stack((grads_one[0], grads_two[0]))
        conv_acc = conv_acc + weight_mask * jnp.stack((grads_one[1], grads_two[1]))
        gain_acc = gain_acc + weight_mask * jnp.stack((grads_one[2], grads_two[2]))
        bias_acc = bias_acc + weight_mask * jnp.stack((grads_one[3], grads_two[3]))
        current = lax.dynamic_index_in_dim(latent[0], safe_mb, 0, keepdims=False)
        kept = jnp.where(is_valid, out_grad, current)
        latent = lax.dynamic_update_index_in_dim(latent, kept[None, None], safe_mb, 1)
        received = passed_along(out_grad, "segment", -1)
        return (received, latent, proj_acc, conv_acc, gain_acc, bias_acc)

    final = lax.fori_loop(0, ticks, one_tick, initial)
    latent = final[1]
    proj_sum, conv_sum, gain_sum, bias_sum = lax.psum(
        (final[2], final[3], final[4], final[5]), "dp"
    )
    return (latent, proj_sum[None], conv_sum[None], gain_sum[None], bias_sum[None])


def solution(mesh):
    return jax.shard_map(
        per_device,
        mesh=mesh,
        in_specs=(
            P("dp", None, "chan"),
            P("segment", "dp", "chan", None),
            P("segment", "dp", "chan", None),
            P("segment", "dp", "chan", None),
            P("segment", "dp", "chan", None),
            P("segment", None, "chan", None),
            P("segment", None, "chan", None),
            P("segment", None, "chan"),
            P("segment", None, "chan"),
        ),
        out_specs=(
            P("segment", "dp", None, "chan"),
            P("segment", None, "chan", None),
            P("segment", None, "chan", None),
            P("segment", None, "chan"),
            P("segment", None, "chan"),
        ),
        check_vma=False,
    )
```

profile of v0, /device:TPU:2, one launch (start us, length us, event | category | flops | bytes accessed | tf_op | source)
XLA Modules:
  0.0 469.4 jit_solution(2428649469921807830)
XLA Ops:
  7.3 1.8 copy.64
  9.6 357.8 %while.26 = (s32[]{:T(128)}, bf16[1536,16]{0,1:T(8,128)(2,1)S(1)}, bf16[1,1,1536,16]{2,3,1,0:T(8,128)(2,1)}, f32[2,96,1536]{2,1,0:T(8,128)S(1)}, f32[2,96,432]{1...) while((s32[]{:T(128)}, bf16[1536,16]{0,1:T(8,128)(2,1)S(1)}, ...), condition=%wide.region_21.22_spmd.clone, body=%wide.region_0.21_spmd.clone.sunk | while | flops 392720768 | bytes 27672152 | solution.py:158
  11.2 0.9 convert_reduce_fusion.5
  12.5 1.0 multiply_reduce_fusion.13
  14.7 19.7 %all_gather.24 = bf16[1536,256]{0,1:T(8,128)(2,1)S(1)} all-gather(bf16[1536,16]{0,1:T(8,128)(2,1)S(1)} %bitcast_select_fusion.3), channel_id=1, replica_groups=mesh['segment'=4,'chan'=16,'dp'=8] {'chan'}, dimensions={1}, use_global_device_ids=true | all-gather | bytes 835584 | tf_op jit(solution)/shard_map/while/body/eval_jaxpr/all_gather | solution.py:81
  34.4 2.0 multiply_reduce_fusion.14
  37.0 1.0 fusion.353
  40.7 4.4 all-to-all-start
  52.0 1.0 all-to-all-done
  53.2 18.4 %all_gather.25 = bf16[1536,256]{0,1:T(8,128)(2,1)S(1)} all-gather(bf16[1536,16]{0,1:T(8,128)(2,1)S(1)} %add_convert_fusion.4), channel_id=1, replica_groups=mesh['segment'=4,'chan'=16,'dp'=8] {'chan'}, dimensions={1}, use_global_device_ids=true | all-gather | bytes 835584 | tf_op jit(solution)/shard_map/while/body/eval_jaxpr/all_gather | solution.py:81
  71.6 2.0 multiply_reduce_fusion.15
  76.8 4.6 all-to-all-start.1
  81.5 0.8 fusion.369
  88.9 1.2 copy.167
  91.7 1.4 fusion.358
  93.2 3.9 collective-permute-start
  97.2 1.9 collective-permute-done
  100.8 0.9 convert_reduce_fusion.5
  102.1 1.0 multiply_reduce_fusion.13
  104.2 19.4 %all_gather.24 = bf16[1536,256]{0,1:T(8,128)(2,1)S(1)} all-gather(bf16[1536,16]{0,1:T(8,128)(2,1)S(1)} %bitcast_select_fusion.3), channel_id=1, replica_groups=mesh['segment'=4,'chan'=16,'dp'=8] {'chan'}, dimensions={1}, use_global_device_ids=true | all-gather | bytes 835584 | tf_op jit(solution)/shard_map/while/body/eval_jaxpr/all_gather | solution.py:81
  123.6 2.0 multiply_reduce_fusion.14
  126.2 1.0 fusion.353
  129.9 4.6 all-to-all-start
  141.4 1.0 all-to-all-done
  142.6 18.4 %all_gather.25 = bf16[1536,256]{0,1:T(8,128)(2,1)S(1)} all-gather(bf16[1536,16]{0,1:T(8,128)(2,1)S(1)} %add_convert_fusion.4), channel_id=1, replica_groups=mesh['segment'=4,'chan'=16,'dp'=8] {'chan'}, dimensions={1}, use_global_device_ids=true | all-gather | bytes 835584 | tf_op jit(solution)/shard_map/while/body/eval_jaxpr/all_gather | solution.py:81
  161.0 2.0 multiply_reduce_fusion.15
  166.3 4.6 all-to-all-start.1
  170.9 0.8 fusion.369
  178.3 1.2 copy.167
  181.2 1.4 fusion.358
  182.6 3.9 collective-permute-start
  186.6 1.9 collective-permute-done
  190.2 0.9 convert_reduce_fusion.5
  191.5 1.0 multiply_reduce_fusion.13
  193.7 19.4 %all_gather.24 = bf16[1536,256]{0,1:T(8,128)(2,1)S(1)} all-gather(bf16[1536,16]{0,1:T(8,128)(2,1)S(1)} %bitcast_select_fusion.3), channel_id=1, replica_groups=mesh['segment'=4,'chan'=16,'dp'=8] {'chan'}, dimensions={1}, use_global_device_ids=true | all-gather | bytes 835584 | tf_op jit(solution)/shard_map/while/body/eval_jaxpr/all_gather | solution.py:81
  213.1 2.0 multiply_reduce_fusion.14
  215.7 1.0 fusion.353
  219.4 4.6 all-to-all-start
  230.9 1.0 all-to-all-done
  232.1 18.4 %all_gather.25 = bf16[1536,256]{0,1:T(8,128)(2,1)S(1)} all-gather(bf16[1536,16]{0,1:T(8,128)(2,1)S(1)} %add_convert_fusion.4), channel_id=1, replica_groups=mesh['segment'=4,'chan'=16,'dp'=8] {'chan'}, dimensions={1}, use_global_device_ids=true | all-gather | bytes 835584 | tf_op jit(solution)/shard_map/while/body/eval_jaxpr/all_gather | solution.py:81
  250.5 2.0 multiply_reduce_fusion.15
  255.7 4.6 all-to-all-start.1
  267.8 1.2 copy.167
  270.6 1.4 fusion.358
  272.1 3.9 collective-permute-start
  276.1 1.9 collective-permute-done
  279.7 0.9 convert_reduce_fusion.5
  280.9 1.0 multiply_reduce_fusion.13
  283.1 19.4 %all_gather.24 = bf16[1536,256]{0,1:T(8,128)(2,1)S(1)} all-gather(bf16[1536,16]{0,1:T(8,128)(2,1)S(1)} %bitcast_select_fusion.3), channel_id=1, replica_groups=mesh['segment'=4,'chan'=16,'dp'=8] {'chan'}, dimensions={1}, use_global_device_ids=true | all-gather | bytes 835584 | tf_op jit(solution)/shard_map/while/body/eval_jaxpr/all_gather | solution.py:81
  302.5 2.0 multiply_reduce_fusion.14
  305.1 1.0 fusion.353
  308.8 4.6 all-to-all-start
  320.3 1.0 all-to-all-done
  321.5 18.4 %all_gather.25 = bf16[1536,256]{0,1:T(8,128)(2,1)S(1)} all-gather(bf16[1536,16]{0,1:T(8,128)(2,1)S(1)} %add_convert_fusion.4), channel_id=1, replica_groups=mesh['segment'=4,'chan'=16,'dp'=8] {'chan'}, dimensions={1}, use_global_device_ids=true | all-gather | bytes 835584 | tf_op jit(solution)/shard_map/while/body/eval_jaxpr/all_gather | solution.py:81
  339.9 2.0 multiply_reduce_fusion.15
  345.1 4.6 all-to-all-start.1
  357.2 1.2 copy.167
  360.0 1.4 fusion.358
  361.5 3.9 collective-permute-start
  365.5 1.9 collective-permute-done
  367.5 2.4 copy.65
  369.9 23.8 %all-reduce.18 = (f32[1,2,96]{2,1,0:T(2,128)}, f32[1,2,96]{2,1,0:T(2,128)}) all-reduce(f32[1,2,96]{2,1,0:T(2,128)S(1)} %bitcast.586, f32[1,2,96]{2,1,0:T(2,128)S(1)} %bitcast.587), channel_id=1, replica_groups=mesh['segment'=4,'chan'=16,'dp'=8] {'dp'}, use_global_device_ids=true, to_apply=%region_24.25 | all-reduce | flops 384 | bytes 3072 | tf_op jit(solution)/shard_map/psum | solution.py:160
  393.7 65.7 %all-reduce.22.cloned.1.call-done = (f32[1,2,96,1536]{3,2,1,0:T(8,128)}, f32[1,2,96,432]{3,2,1,0:T(8,128)}) async-done(((f32[1,2,96,1536]{3,2,1,0:T(8,128)}, f32[1,2,96,432]{3,2,1,0:T(8,128)}), (f32[1,2,96,1536]{3,2,1,0:T(8,128)}, f32[1,2,96,432]{3,2,1,0:T(8,128)})) %all-reduce.22.cloned.1.call-update) | async-done | bytes 1511440 | tf_op jit(solution)/shard_map/psum | solution.py:160
  459.4 2.4 copy.207
  (667 shorter events, 101.1 us)
Async XLA Ops:
  7.2 452.2 %all-reduce.22.cloned.1.call-start = ((), (), s32[]{:S(2)}) async-start(), calls=%async_computation.2 | async-start | bytes 3145728 | tf_op jit(solution)/shard_map/psum | solution.py:160
  9.7 29.8 %copy-start.30 = (pred[256]{0:T(512)(128)(4,1)}, pred[256]{0:T(512)(128)(4,1)S(1)}, u32[]{:S(2)}) copy-start(pred[256]{0:T(512)(128)(4,1)S(1)} %compare_and_fusion.7) | copy-start | bytes 772 | tf_op jit(solution)/shard_map/while
  9.7 29.8 %copy-start.27 = (pred[256]{0:T(512)(128)(4,1)}, pred[256]{0:T(512)(128)(4,1)S(1)}, u32[]{:S(2)}) copy-start(pred[256]{0:T(512)(128)(4,1)S(1)} %compare_and_fusion.8) | copy-start | bytes 772 | tf_op jit(solution)/shard_map/while
  38.8 6.3 %copy-start.2 = (bf16[1,1,96,256]{3,2,1,0:T(8,128)(2,1)S(1)}, bf16[1,1,96,256]{3,2,1,0:T(8,128)(2,1)}, u32[]{:S(2)}) copy-start(bf16[1,1,96,256]{3,2,1,0:T(8,128)(2,1)} %get-tuple-element.854) | copy-start | bytes 147460 | tf_op jit(solution)/shard_map/while
  39.5 9.8 %copy-start.7 = (bf16[1,1,96,256]{3,2,1,0:T(8,128)(2,1)S(1)}, bf16[1,1,96,256]{3,2,1,0:T(8,128)(2,1)}, u32[]{:S(2)}) copy-start(bf16[1,1,96,256]{3,2,1,0:T(8,128)(2,1)} %get-tuple-element.857) | copy-start | bytes 147460 | tf_op jit(solution)/shard_map/while
  39.8 9.5 %copy-start.31 = (pred[256]{0:T(512)(128)(4,1)S(1)}, pred[256]{0:T(512)(128)(4,1)}, u32[]{:S(2)}) copy-start(pred[256]{0:T(512)(128)(4,1)} %copy-done.30) | copy-start | bytes 772 | tf_op jit(solution)/shard_map/while
  39.8 9.9 %copy-start.28 = (pred[256]{0:T(512)(128)(4,1)S(1)}, pred[256]{0:T(512)(128)(4,1)}, u32[]{:S(2)}) copy-start(pred[256]{0:T(512)(128)(4,1)} %copy-done.27) | copy-start | bytes 772 | tf_op jit(solution)/shard_map/while
  40.7 12.3 %all-to-all-start = ((bf16[96,16,16]{0,2,1:T(8,128)(2,1)}), bf16[96,16,16]{0,2,1:T(8,128)(2,1)S(1)}, u32[]{:S(2)}, u32[]{:S(2)}) async-start(bf16[96,16,16]{0,2,1:T(8,128)(2,1)} %convert_element_type.430), calls=%async_computation | async-start | bytes 131072 | tf_op jit(solution)/shard_map/while/body/eval_jaxpr/all_to_all | solution.py:87
  52.0 19.6 %copy-start.22 = (f32[96]{0:T(128)S(1)}, f32[96]{0:T(128)}, u32[]{:S(2)}) copy-start(f32[96]{0:T(128)} %mul.953) | copy-start | bytes 1156 | tf_op jit(solution)/shard_map/while
  75.0 6.5 %copy-start.6 = (bf16[1,1,96,256]{3,2,1,0:T(8,128)(2,1)S(1)}, bf16[1,1,96,256]{3,2,1,0:T(8,128)(2,1)}, u32[]{:S(2)}) copy-start(bf16[1,1,96,256]{3,2,1,0:T(8,128)(2,1)} %get-tuple-element.856) | copy-start | bytes 147460 | tf_op jit(solution)/shard_map/while
  76.8 14.7 %all-to-all-start.1 = ((bf16[96,16,16]{0,2,1:T(8,128)(2,1)}), bf16[96,16,16]{0,2,1:T(8,128)(2,1)S(1)}, u32[]{:S(2)}, u32[]{:S(2)}) async-start(bf16[96,16,16]{0,2,1:T(8,128)(2,1)} %convert_element_type.431), calls=%async_computation.1 | async-start | bytes 131072 | tf_op jit(solution)/shard_map/while/body/eval_jaxpr/all_to_all | solution.py:87
  90.8 6.3 %copy-start.10 = (f32[2,96]{1,0:T(2,128)S(1)}, f32[2,96]{1,0:T(2,128)}, u32[]{:S(2)}) copy-start(f32[2,96]{1,0:T(2,128)} %get-tuple-element.824) | copy-start | bytes 2308 | tf_op jit(solution)/shard_map/while
  90.8 6.3 %copy-start.13 = (f32[2,96]{1,0:T(2,128)S(1)}, f32[2,96]{1,0:T(2,128)}, u32[]{:S(2)}) copy-start(f32[2,96]{1,0:T(2,128)} %get-tuple-element.825) | copy-start | bytes 2308 | tf_op jit(solution)/shard_map/while
  90.8 6.3 %copy-start.23 = (f32[96]{0:T(128)S(1)}, f32[96]{0:T(128)}, u32[]{:S(2)}) copy-start(f32[96]{0:T(128)} %get-tuple-element.792) | copy-start | bytes 1156 | tf_op jit(solution)/shard_map/while
  90.8 6.3 %copy-start.24 = (f32[96]{0:T(128)S(1)}, f32[96]{0:T(128)}, u32[]{:S(2)}) copy-start(f32[96]{0:T(128)} %get-tuple-element.794) | copy-start | bytes 1156 | tf_op jit(solution)/shard_map/while
  90.8 6.3 %copy-start.25 = (f32[96]{0:T(128)S(1)}, f32[96]{0:T(128)}, u32[]{:S(2)}) copy-start(f32[96]{0:T(128)} %get-tuple-element.793) | copy-start | bytes 1156 | tf_op jit(solution)/shard_map/while
  90.9 6.3 %copy-start.26 = (f32[96]{0:T(128)S(1)}, f32[96]{0:T(128)}, u32[]{:S(2)}) copy-start(f32[96]{0:T(128)} %get-tuple-element.795) | copy-start | bytes 1156 | tf_op jit(solution)/shard_map/while
  91.5 7.6 %copy-start.4 = (f32[2,96,432]{1,2,0:T(8,128)}, f32[2,96,432]{1,2,0:T(8,128)S(1)}, u32[]{:S(2)}) copy-start(f32[2,96,432]{1,2,0:T(8,128)S(1)} %fusion.378) | copy-start | bytes 995332 | tf_op jit(solution)/shard_map/while
  93.2 6.0 %collective-permute-start = (bf16[1536,16]{0,1:T(8,128)(2,1)S(1)}, bf16[1536,16]{0,1:T(8,128)(2,1)S(1)}, u32[]{:S(2)}, u32[]{:S(2)}) collective-permute-start(bf16[1536,16]{0,1:T(8,128)(2,1)S(1)} %get-tuple-element.790), channel_id=1, source_target_pairs={{128,0},{256,128},{384,256},{129,1},{257,129},{385,257},{130,2},{2... | collective-permute-start | bytes 147464 | tf_op jit(solution)/shard_map/while/body/eval_jaxpr/ppermute | solution.py:14
  99.2 29.5 %copy-start.30 = (pred[256]{0:T(512)(128)(4,1)}, pred[256]{0:T(512)(128)(4,1)S(1)}, u32[]{:S(2)}) copy-start(pred[256]{0:T(512)(128)(4,1)S(1)} %compare_and_fusion.7) | copy-start | bytes 772 | tf_op jit(solution)/shard_map/while
  99.2 29.5 %copy-start.27 = (pred[256]{0:T(512)(128)(4,1)}, pred[256]{0:T(512)(128)(4,1)S(1)}, u32[]{:S(2)}) copy-start(pred[256]{0:T(512)(128)(4,1)S(1)} %compare_and_fusion.8) | copy-start | bytes 772 | tf_op jit(solution)/shard_map/while
  128.0 6.5 %copy-start.2 = (bf16[1,1,96,256]{3,2,1,0:T(8,128)(2,1)S(1)}, bf16[1,1,96,256]{3,2,1,0:T(8,128)(2,1)}, u32[]{:S(2)}) copy-start(bf16[1,1,96,256]{3,2,1,0:T(8,128)(2,1)} %get-tuple-element.854) | copy-start | bytes 147460 | tf_op jit(solution)/shard_map/while
  128.7 10.0 %copy-start.7 = (bf16[1,1,96,256]{3,2,1,0:T(8,128)(2,1)S(1)}, bf16[1,1,96,256]{3,2,1,0:T(8,128)(2,1)}, u32[]{:S(2)}) copy-start(bf16[1,1,96,256]{3,2,1,0:T(8,128)(2,1)} %get-tuple-element.857) | copy-start | bytes 147460 | tf_op jit(solution)/shard_map/while
  129.0 9.7 %copy-start.31 = (pred[256]{0:T(512)(128)(4,1)S(1)}, pred[256]{0:T(512)(128)(4,1)}, u32[]{:S(2)}) copy-start(pred[256]{0:T(512)(128)(4,1)} %copy-done.30) | copy-start | bytes 772 | tf_op jit(solution)/shard_map/while
  129.0 10.1 %copy-start.28 = (pred[256]{0:T(512)(128)(4,1)S(1)}, pred[256]{0:T(512)(128)(4,1)}, u32[]{:S(2)}) copy-start(pred[256]{0:T(512)(128)(4,1)} %copy-done.27) | copy-start | bytes 772 | tf_op jit(solution)/shard_map/while
  129.9 12.5 %all-to-all-start = ((bf16[96,16,16]{0,2,1:T(8,128)(2,1)}), bf16[96,16,16]{0,2,1:T(8,128)(2,1)S(1)}, u32[]{:S(2)}, u32[]{:S(2)}) async-start(bf16[96,16,16]{0,2,1:T(8,128)(2,1)} %convert_element_type.430), calls=%async_computation | async-start | bytes 131072 | tf_op jit(solution)/shard_map/while/body/eval_jaxpr/all_to_all | solution.py:87
  141.4 19.6 %copy-start.22 = (f32[96]{0:T(128)S(1)}, f32[96]{0:T(128)}, u32[]{:S(2)}) copy-start(f32[96]{0:T(128)} %mul.953) | copy-start | bytes 1156 | tf_op jit(solution)/shard_map/while
  164.4 6.5 %copy-start.6 = (bf16[1,1,96,256]{3,2,1,0:T(8,128)(2,1)S(1)}, bf16[1,1,96,256]{3,2,1,0:T(8,128)(2,1)}, u32[]{:S(2)}) copy-start(bf16[1,1,96,256]{3,2,1,0:T(8,128)(2,1)} %get-tuple-element.856) | copy-start | bytes 147460 | tf_op jit(solution)/shard_map/while
  166.3 14.7 %all-to-all-start.1 = ((bf16[96,16,16]{0,2,1:T(8,128)(2,1)}), bf16[96,16,16]{0,2,1:T(8,128)(2,1)S(1)}, u32[]{:S(2)}, u32[]{:S(2)}) async-start(bf16[96,16,16]{0,2,1:T(8,128)(2,1)} %convert_element_type.431), calls=%async_computation.1 | async-start | bytes 131072 | tf_op jit(solution)/shard_map/while/body/eval_jaxpr/all_to_all | solution.py:87
  180.2 6.3 %copy-start.10 = (f32[2,96]{1,0:T(2,128)S(1)}, f32[2,96]{1,0:T(2,128)}, u32[]{:S(2)}) copy-start(f32[2,96]{1,0:T(2,128)} %get-tuple-element.824) | copy-start | bytes 2308 | tf_op jit(solution)/shard_map/while
  180.2 6.3 %copy-start.13 = (f32[2,96]{1,0:T(2,128)S(1)}, f32[2,96]{1,0:T(2,128)}, u32[]{:S(2)}) copy-start(f32[2,96]{1,0:T(2,128)} %get-tuple-element.825) | copy-start | bytes 2308 | tf_op jit(solution)/shard_map/while
  180.3 6.3 %copy-start.23 = (f32[96]{0:T(128)S(1)}, f32[96]{0:T(128)}, u32[]{:S(2)}) copy-start(f32[96]{0:T(128)} %get-tuple-element.792) | copy-start | bytes 1156 | tf_op jit(solution)/shard_map/while
  180.3 6.3 %copy-start.24 = (f32[96]{0:T(128)S(1)}, f32[96]{0:T(128)}, u32[]{:S(2)}) copy-start(f32[96]{0:T(128)} %get-tuple-element.794) | copy-start | bytes 1156 | tf_op jit(solution)/shard_map/while
  180.3 6.3 %copy-start.25 = (f32[96]{0:T(128)S(1)}, f32[96]{0:T(128)}, u32[]{:S(2)}) copy-start(f32[96]{0:T(128)} %get-tuple-element.793) | copy-start | bytes 1156 | tf_op jit(solution)/shard_map/while
  181.0 7.6 %copy-start.4 = (f32[2,96,432]{1,2,0:T(8,128)}, f32[2,96,432]{1,2,0:T(8,128)S(1)}, u32[]{:S(2)}) copy-start(f32[2,96,432]{1,2,0:T(8,128)S(1)} %fusion.378) | copy-start | bytes 995332 | tf_op jit(solution)/shard_map/while
  182.6 6.0 %collective-permute-start = (bf16[1536,16]{0,1:T(8,128)(2,1)S(1)}, bf16[1536,16]{0,1:T(8,128)(2,1)S(1)}, u32[]{:S(2)}, u32[]{:S(2)}) collective-permute-start(bf16[1536,16]{0,1:T(8,128)(2,1)S(1)} %get-tuple-element.790), channel_id=1, source_target_pairs={{128,0},{256,128},{384,256},{129,1},{257,129},{385,257},{130,2},{2... | collective-permute-start | bytes 147464 | tf_op jit(solution)/shard_map/while/body/eval_jaxpr/ppermute | solution.py:14
  188.6 29.5 %copy-start.30 = (pred[256]{0:T(512)(128)(4,1)}, pred[256]{0:T(512)(128)(4,1)S(1)}, u32[]{:S(2)}) copy-start(pred[256]{0:T(512)(128)(4,1)S(1)} %compare_and_fusion.7) | copy-start | bytes 772 | tf_op jit(solution)/shard_map/while
  188.7 29.5 %copy-start.27 = (pred[256]{0:T(512)(128)(4,1)}, pred[256]{0:T(512)(128)(4,1)S(1)}, u32[]{:S(2)}) copy-start(pred[256]{0:T(512)(128)(4,1)S(1)} %compare_and_fusion.8) | copy-start | bytes 772 | tf_op jit(solution)/shard_map/while
  217.5 6.5 %copy-start.2 = (bf16[1,1,96,256]{3,2,1,0:T(8,128)(2,1)S(1)}, bf16[1,1,96,256]{3,2,1,0:T(8,128)(2,1)}, u32[]{:S(2)}) copy-start(bf16[1,1,96,256]{3,2,1,0:T(8,128)(2,1)} %get-tuple-element.854) | copy-start | bytes 147460 | tf_op jit(solution)/shard_map/while
  218.2 10.0 %copy-start.7 = (bf16[1,1,96,256]{3,2,1,0:T(8,128)(2,1)S(1)}, bf16[1,1,96,256]{3,2,1,0:T(8,128)(2,1)}, u32[]{:S(2)}) copy-start(bf16[1,1,96,256]{3,2,1,0:T(8,128)(2,1)} %get-tuple-element.857) | copy-start | bytes 147460 | tf_op jit(solution)/shard_map/while
  218.5 9.7 %copy-start.31 = (pred[256]{0:T(512)(128)(4,1)S(1)}, pred[256]{0:T(512)(128)(4,1)}, u32[]{:S(2)}) copy-start(pred[256]{0:T(512)(128)(4,1)} %copy-done.30) | copy-start | bytes 772 | tf_op jit(solution)/shard_map/while
  218.5 10.1 %copy-start.28 = (pred[256]{0:T(512)(128)(4,1)S(1)}, pred[256]{0:T(512)(128)(4,1)}, u32[]{:S(2)}) copy-start(pred[256]{0:T(512)(128)(4,1)} %copy-done.27) | copy-start | bytes 772 | tf_op jit(solution)/shard_map/while
  219.4 12.5 %all-to-all-start = ((bf16[96,16,16]{0,2,1:T(8,128)(2,1)}), bf16[96,16,16]{0,2,1:T(8,128)(2,1)S(1)}, u32[]{:S(2)}, u32[]{:S(2)}) async-start(bf16[96,16,16]{0,2,1:T(8,128)(2,1)} %convert_element_type.430), calls=%async_computation | async-start | bytes 131072 | tf_op jit(solution)/shard_map/while/body/eval_jaxpr/all_to_all | solution.py:87
  230.9 19.6 %copy-start.22 = (f32[96]{0:T(128)S(1)}, f32[96]{0:T(128)}, u32[]{:S(2)}) copy-start(f32[96]{0:T(128)} %mul.953) | copy-start | bytes 1156 | tf_op jit(solution)/shard_map/while
  253.8 6.5 %copy-start.6 = (bf16[1,1,96,256]{3,2,1,0:T(8,128)(2,1)S(1)}, bf16[1,1,96,256]{3,2,1,0:T(8,128)(2,1)}, u32[]{:S(2)}) copy-start(bf16[1,1,96,256]{3,2,1,0:T(8,128)(2,1)} %get-tuple-element.856) | copy-start | bytes 147460 | tf_op jit(solution)/shard_map/while
  255.7 14.7 %all-to-all-start.1 = ((bf16[96,16,16]{0,2,1:T(8,128)(2,1)}), bf16[96,16,16]{0,2,1:T(8,128)(2,1)S(1)}, u32[]{:S(2)}, u32[]{:S(2)}) async-start(bf16[96,16,16]{0,2,1:T(8,128)(2,1)} %convert_element_type.431), calls=%async_computation.1 | async-start | bytes 131072 | tf_op jit(solution)/shard_map/while/body/eval_jaxpr/all_to_all | solution.py:87
  269.7 6.3 %copy-start.10 = (f32[2,96]{1,0:T(2,128)S(1)}, f32[2,96]{1,0:T(2,128)}, u32[]{:S(2)}) copy-start(f32[2,96]{1,0:T(2,128)} %get-tuple-element.824) | copy-start | bytes 2308 | tf_op jit(solution)/shard_map/while
  269.7 6.3 %copy-start.13 = (f32[2,96]{1,0:T(2,128)S(1)}, f32[2,96]{1,0:T(2,128)}, u32[]{:S(2)}) copy-start(f32[2,96]{1,0:T(2,128)} %get-tuple-element.825) | copy-start | bytes 2308 | tf_op jit(solution)/shard_map/while
  270.4 7.6 %copy-start.4 = (f32[2,96,432]{1,2,0:T(8,128)}, f32[2,96,432]{1,2,0:T(8,128)S(1)}, u32[]{:S(2)}) copy-start(f32[2,96,432]{1,2,0:T(8,128)S(1)} %fusion.378) | copy-start | bytes 995332 | tf_op jit(solution)/shard_map/while
  272.1 6.0 %collective-permute-start = (bf16[1536,16]{0,1:T(8,128)(2,1)S(1)}, bf16[1536,16]{0,1:T(8,128)(2,1)S(1)}, u32[]{:S(2)}, u32[]{:S(2)}) collective-permute-start(bf16[1536,16]{0,1:T(8,128)(2,1)S(1)} %get-tuple-element.790), channel_id=1, source_target_pairs={{128,0},{256,128},{384,256},{129,1},{257,129},{385,257},{130,2},{2... | collective-permute-start | bytes 147464 | tf_op jit(solution)/shard_map/while/body/eval_jaxpr/ppermute | solution.py:14
  278.1 29.5 %copy-start.30 = (pred[256]{0:T(512)(128)(4,1)}, pred[256]{0:T(512)(128)(4,1)S(1)}, u32[]{:S(2)}) copy-start(pred[256]{0:T(512)(128)(4,1)S(1)} %compare_and_fusion.7) | copy-start | bytes 772 | tf_op jit(solution)/shard_map/while
  278.1 29.5 %copy-start.27 = (pred[256]{0:T(512)(128)(4,1)}, pred[256]{0:T(512)(128)(4,1)S(1)}, u32[]{:S(2)}) copy-start(pred[256]{0:T(512)(128)(4,1)S(1)} %compare_and_fusion.8) | copy-start | bytes 772 | tf_op jit(solution)/shard_map/while
  306.9 6.5 %copy-start.2 = (bf16[1,1,96,256]{3,2,1,0:T(8,128)(2,1)S(1)}, bf16[1,1,96,256]{3,2,1,0:T(8,128)(2,1)}, u32[]{:S(2)}) copy-start(bf16[1,1,96,256]{3,2,1,0:T(8,128)(2,1)} %get-tuple-element.854) | copy-start | bytes 147460 | tf_op jit(solution)/shard_map/while
  307.6 10.0 %copy-start.7 = (bf16[1,1,96,256]{3,2,1,0:T(8,128)(2,1)S(1)}, bf16[1,1,96,256]{3,2,1,0:T(8,128)(2,1)}, u32[]{:S(2)}) copy-start(bf16[1,1,96,256]{3,2,1,0:T(8,128)(2,1)} %get-tuple-element.857) | copy-start | bytes 147460 | tf_op jit(solution)/shard_map/while
  307.9 9.7 %copy-start.31 = (pred[256]{0:T(512)(128)(4,1)S(1)}, pred[256]{0:T(512)(128)(4,1)}, u32[]{:S(2)}) copy-start(pred[256]{0:T(512)(128)(4,1)} %copy-done.30) | copy-start | bytes 772 | tf_op jit(solution)/shard_map/while
  307.9 10.1 %copy-start.28 = (pred[256]{0:T(512)(128)(4,1)S(1)}, pred[256]{0:T(512)(128)(4,1)}, u32[]{:S(2)}) copy-start(pred[256]{0:T(512)(128)(4,1)} %copy-done.27) | copy-start | bytes 772 | tf_op jit(solution)/shard_map/while
  308.8 12.5 %all-to-all-start = ((bf16[96,16,16]{0,2,1:T(8,128)(2,1)}), bf16[96,16,16]{0,2,1:T(8,128)(2,1)S(1)}, u32[]{:S(2)}, u32[]{:S(2)}) async-start(bf16[96,16,16]{0,2,1:T(8,128)(2,1)} %convert_element_type.430), calls=%async_computation | async-start | bytes 131072 | tf_op jit(solution)/shard_map/while/body/eval_jaxpr/all_to_all | solution.py:87
  320.3 19.6 %copy-start.22 = (f32[96]{0:T(128)S(1)}, f32[96]{0:T(128)}, u32[]{:S(2)}) copy-start(f32[96]{0:T(128)} %mul.953) | copy-start | bytes 1156 | tf_op jit(solution)/shard_map/while
  343.3 6.5 %copy-start.6 = (bf16[1,1,96,256]{3,2,1,0:T(8,128)(2,1)S(1)}, bf16[1,1,96,256]{3,2,1,0:T(8,128)(2,1)}, u32[]{:S(2)}) copy-start(bf16[1,1,96,256]{3,2,1,0:T(8,128)(2,1)} %get-tuple-element.856) | copy-start | bytes 147460 | tf_op jit(solution)/shard_map/while
  345.1 14.7 %all-to-all-start.1 = ((bf16[96,16,16]{0,2,1:T(8,128)(2,1)}), bf16[96,16,16]{0,2,1:T(8,128)(2,1)S(1)}, u32[]{:S(2)}, u32[]{:S(2)}) async-start(bf16[96,16,16]{0,2,1:T(8,128)(2,1)} %convert_element_type.431), calls=%async_computation.1 | async-start | bytes 131072 | tf_op jit(solution)/shard_map/while/body/eval_jaxpr/all_to_all | solution.py:87
  359.1 6.3 %copy-start.10 = (f32[2,96]{1,0:T(2,128)S(1)}, f32[2,96]{1,0:T(2,128)}, u32[]{:S(2)}) copy-start(f32[2,96]{1,0:T(2,128)} %get-tuple-element.824) | copy-start | bytes 2308 | tf_op jit(solution)/shard_map/while
  359.1 6.3 %copy-start.13 = (f32[2,96]{1,0:T(2,128)S(1)}, f32[2,96]{1,0:T(2,128)}, u32[]{:S(2)}) copy-start(f32[2,96]{1,0:T(2,128)} %get-tuple-element.825) | copy-start | bytes 2308 | tf_op jit(solution)/shard_map/while
  359.8 7.6 %copy-start.4 = (f32[2,96,432]{1,2,0:T(8,128)}, f32[2,96,432]{1,2,0:T(8,128)S(1)}, u32[]{:S(2)}) copy-start(f32[2,96,432]{1,2,0:T(8,128)S(1)} %fusion.378) | copy-start | bytes 995332 | tf_op jit(solution)/shard_map/while
  361.5 6.0 %collective-permute-start = (bf16[1536,16]{0,1:T(8,128)(2,1)S(1)}, bf16[1536,16]{0,1:T(8,128)(2,1)S(1)}, u32[]{:S(2)}, u32[]{:S(2)}) collective-permute-start(bf16[1536,16]{0,1:T(8,128)(2,1)S(1)} %get-tuple-element.790), channel_id=1, source_target_pairs={{128,0},{256,128},{384,256},{129,1},{257,129},{385,257},{130,2},{2... | collective-permute-start | bytes 147464 | tf_op jit(solution)/shard_map/while/body/eval_jaxpr/ppermute | solution.py:14
  (69 other events, 161.8 us)
Sparse Core Ops, SparseCore 0:
  370.0 89.2 all-reduce.21
where the time goes:
time: 472 us; the launch traced here: 469 us
  blocking collectives  175 us (37%)
  waiting for transfers between devices  77.5 us (16%)
  matrix products  66.1 us (14%)
  local copies, waits for them, and re-layouts  56 us (12%)
  starting transfers between devices  52.6 us (11%)
  other arithmetic  25.2 us (5%)
  between operations  14.1 us (3%)
    all_gather x8, blocking collectives, block_sharded(): grad_piece = lax.all_gather(grad_slab, 'chan', axis=1, tiled=True)  152 us
    psum x1, waiting for transfers between devices, per_device(): lax.psum((final[2], final[3], final[4], final[5]), 'dp')  65.7 us
    dot_general x72, matrix products, conv_backward(): jnp.einsum('gop,gjp->goj', grad_pre, source, preferred_element_type=jnp.f...  36.9 us
    all_to_all x8, starting transfers between devices, block_sharded(): lax.all_to_all(branch, 'chan', split_axis=1, concat_axis=0, tiled=True)  36.9 us
    psum x1, blocking collectives, per_device(): lax.psum((final[2], final[3], final[4], final[5]), 'dp')  23.8 us
    dot_general x8, matrix products, block_sharded(): fresh = jnp.dot(w_proj, grad_piece, preferred_element_type=jnp.float32)  16 us
    ppermute x4, starting transfers between devices, passed_along(): return lax.ppermute(block, axis, route)  15.7 us
    dot_general x72, matrix products, conv_backward(): jnp.einsum('goj,gop->gjp', taps_w[:, :, tap_at, :], grad_pre, preferred_e...  10.6 us
  transfers between devices with their start and end apart: 13, of which 9 were waited for; matrix products, arithmetic and copies ran while one was open for 13% of the time, Pallas kernels for 0%

commit v1 on v0

--- a/solution.py
+++ b/solution.py
@@ -1,3 +1,4 @@
+import functools
 import jax
 import jax.numpy as jnp
 from jax import lax
@@ -6,6 +7,16 @@
 GS = 48
 WW = 64
 NORM_EPS = 1e-05
+
+
+def link_weights_in(v0, net_axis):
+    return jnp.concatenate(
+        lax.all_to_all(jnp.stack(jnp.split(v0, lax.psum(1, net_axis), 1), axis=0), net_axis, 0, 0),
+        0,
+    )
+
+
+read_trees_up = functools.partial(link_weights_in, net_axis="chan")
 
 
 def passed_along(block, axis, distance):
@@ -84,7 +95,7 @@
         act_bf, grad_piece, (((1,), (1,)), ((), ())), preferred_element_type=jnp.float32
     )
     branch, conv_grad, gain_grad, bias_grad = conv_backward(fresh, norm_state, saved_in, w_conv)
-    returned = lax.all_to_all(branch, "chan", split_axis=1, concat_axis=0, tiled=True)
+    returned = read_trees_up(branch)
     out_slab = (grad_slab.astype(jnp.float32) + returned.astype(jnp.float32)).astype(jnp.bfloat16)
     return (out_slab, (weight_acc, conv_grad, gain_grad, bias_grad))
 

time: 472 us -> 553 us (1.17)
  local copies, waits for them, and re-layouts: 56 us -> 137 us
    while x232 -> x480, local copies, waits for them, and re-layouts: 4.38 us -> 86.2 us
    convert_element_type x16 -> x0, local copies, waits for them, and re-layouts: 6.92 us -> none  [conv_backward(): branch = back_sum.reshape(chans, positions).astype(jnp.bfloat16)]
  transfers between devices with their start and end apart: 13 -> 13, of which waited for: 9 -> 9; matrix products, arithmetic and copies ran while one was open for 13% -> 11% of each run, Pallas kernels for 0% -> 0%
where the time goes in v1:
time: 553 us; the launch traced here: 551 us
  blocking collectives  176 us (32%)
  local copies, waits for them, and re-layouts  137 us (25%)
  waiting for transfers between devices  77.2 us (14%)
  matrix products  66.4 us (12%)
  starting transfers between devices  52.6 us (10%)
  other arithmetic  25.1 us (5%)
  between operations  14.1 us (3%)
    all_gather x8, blocking collectives, block_sharded(): grad_piece = lax.all_gather(grad_slab, 'chan', axis=1, tiled=True)  152 us
    while x480, local copies, waits for them, and re-layouts  86.2 us
    psum x1, waiting for transfers between devices, per_device(): lax.psum((final[2], final[3], final[4], final[5]), 'dp')  65.7 us
    dot_general x72, matrix products, conv_backward(): jnp.einsum('gop,gjp->goj', grad_pre, source, preferred_element_type=jnp.f...  36.9 us
    all_to_all x8, starting transfers between devices, link_weights_in(): lax.all_to_all(jnp.stack(jnp.split(v0, lax.psum(1, net_axis), 1), axis=0)...  36.9 us
    psum x1, blocking collectives, per_device(): lax.psum((final[2], final[3], final[4], final[5]), 'dp')  23.8 us
    dot_general x8, matrix products, block_sharded(): fresh = jnp.dot(w_proj, grad_piece, preferred_element_type=jnp.float32)  16.2 us
    ppermute x4, starting transfers between devices, passed_along(): return lax.ppermute(block, axis, route)  15.7 us
  transfers between devices with their start and end apart: 13, of which 9 were waited for; matrix products, arithmetic and copies ran while one was open for 11% of the time, Pallas kernels for 0%

profile of v1, /device:TPU:2, one launch (start us, length us, event | category | flops | bytes accessed | tf_op | source)
XLA Modules:
  0.0 550.8 jit_solution(8605253235901828258)
XLA Ops:
  7.3 1.8 copy.94
  9.6 439.2 %while.26 = (s32[]{:T(128)}, bf16[1536,16]{0,1:T(8,128)(2,1)S(1)}, bf16[1,1,1536,16]{2,3,1,0:T(8,128)(2,1)}, f32[2,96,1536]{2,1,0:T(8,128)S(1)}, f32[2,96,432]{1...) while((s32[]{:T(128)}, bf16[1536,16]{0,1:T(8,128)(2,1)S(1)}, ...), condition=%wide.region_21.22_spmd.clone, body=%wide.region_0.21_spmd.clone.sunk | while | flops 392671616 | bytes 27508312 | solution.py:169
  11.2 0.9 convert_reduce_fusion.5
  12.5 1.0 multiply_reduce_fusion.13
  14.7 19.7 %all_gather.24 = bf16[1536,256]{0,1:T(8,128)(2,1)S(1)} all-gather(bf16[1536,16]{0,1:T(8,128)(2,1)S(1)} %bitcast_select_fusion.3), channel_id=1, replica_groups=mesh['segment'=4,'chan'=16,'dp'=8] {'chan'}, dimensions={1}, use_global_device_ids=true | all-gather | bytes 835584 | tf_op jit(solution)/shard_map/while/body/eval_jaxpr/all_gather | solution.py:92
  34.4 2.0 multiply_reduce_fusion.14
  37.0 1.0 fusion.357
  50.9 4.4 all-to-all-start
  62.2 0.9 all-to-all-done
  63.3 18.5 %all_gather.25 = bf16[1536,256]{0,1:T(8,128)(2,1)S(1)} all-gather(bf16[1536,16]{0,1:T(8,128)(2,1)S(1)} %add_convert_fusion.4), channel_id=1, replica_groups=mesh['segment'=4,'chan'=16,'dp'=8] {'chan'}, dimensions={1}, use_global_device_ids=true | all-gather | bytes 835584 | tf_op jit(solution)/shard_map/while/body/eval_jaxpr/all_gather | solution.py:92
  81.8 2.0 multiply_reduce_fusion.15
  97.2 4.6 all-to-all-start.1
  101.9 0.8 fusion.375
  109.3 1.2 copy.289
  112.1 1.5 fusion.364
  113.5 3.9 collective-permute-start
  117.6 1.9 collective-permute-done
  121.1 0.9 convert_reduce_fusion.5
  122.4 1.0 multiply_reduce_fusion.13
  124.6 19.4 %all_gather.24 = bf16[1536,256]{0,1:T(8,128)(2,1)S(1)} all-gather(bf16[1536,16]{0,1:T(8,128)(2,1)S(1)} %bitcast_select_fusion.3), channel_id=1, replica_groups=mesh['segment'=4,'chan'=16,'dp'=8] {'chan'}, dimensions={1}, use_global_device_ids=true | all-gather | bytes 835584 | tf_op jit(solution)/shard_map/while/body/eval_jaxpr/all_gather | solution.py:92
  144.0 2.0 multiply_reduce_fusion.14
  146.6 1.0 fusion.357
  160.4 4.6 all-to-all-start
  172.0 0.9 all-to-all-done
  173.1 18.5 %all_gather.25 = bf16[1536,256]{0,1:T(8,128)(2,1)S(1)} all-gather(bf16[1536,16]{0,1:T(8,128)(2,1)S(1)} %add_convert_fusion.4), channel_id=1, replica_groups=mesh['segment'=4,'chan'=16,'dp'=8] {'chan'}, dimensions={1}, use_global_device_ids=true | all-gather | bytes 835584 | tf_op jit(solution)/shard_map/while/body/eval_jaxpr/all_gather | solution.py:92
  191.6 2.0 multiply_reduce_fusion.15
  207.0 4.6 all-to-all-start.1
  211.6 0.8 fusion.375
  219.1 1.2 copy.289
  221.9 1.5 fusion.364
  223.3 3.9 collective-permute-start
  227.3 1.9 collective-permute-done
  230.9 0.9 convert_reduce_fusion.5
  232.2 1.0 multiply_reduce_fusion.13
  234.4 19.4 %all_gather.24 = bf16[1536,256]{0,1:T(8,128)(2,1)S(1)} all-gather(bf16[1536,16]{0,1:T(8,128)(2,1)S(1)} %bitcast_select_fusion.3), channel_id=1, replica_groups=mesh['segment'=4,'chan'=16,'dp'=8] {'chan'}, dimensions={1}, use_global_device_ids=true | all-gather | bytes 835584 | tf_op jit(solution)/shard_map/while/body/eval_jaxpr/all_gather | solution.py:92
  253.8 2.0 multiply_reduce_fusion.14
  256.4 1.0 fusion.357
  270.2 4.6 all-to-all-start
  281.8 0.9 all-to-all-done
  282.9 18.5 %all_gather.25 = bf16[1536,256]{0,1:T(8,128)(2,1)S(1)} all-gather(bf16[1536,16]{0,1:T(8,128)(2,1)S(1)} %add_convert_fusion.4), channel_id=1, replica_groups=mesh['segment'=4,'chan'=16,'dp'=8] {'chan'}, dimensions={1}, use_global_device_ids=true | all-gather | bytes 835584 | tf_op jit(solution)/shard_map/while/body/eval_jaxpr/all_gather | solution.py:92
  301.4 2.0 multiply_reduce_fusion.15
  316.8 4.6 all-to-all-start.1
  328.9 1.2 copy.289
  331.6 1.5 fusion.364
  333.1 3.9 collective-permute-start
  337.1 1.9 collective-permute-done
  340.7 0.9 convert_reduce_fusion.5
  342.0 1.0 multiply_reduce_fusion.13
  344.2 19.4 %all_gather.24 = bf16[1536,256]{0,1:T(8,128)(2,1)S(1)} all-gather(bf16[1536,16]{0,1:T(8,128)(2,1)S(1)} %bitcast_select_fusion.3), channel_id=1, replica_groups=mesh['segment'=4,'chan'=16,'dp'=8] {'chan'}, dimensions={1}, use_global_device_ids=true | all-gather | bytes 835584 | tf_op jit(solution)/shard_map/while/body/eval_jaxpr/all_gather | solution.py:92
  363.6 2.0 multiply_reduce_fusion.14
  366.1 1.0 fusion.357
  380.0 4.6 all-to-all-start
  391.6 0.9 all-to-all-done
  392.7 18.5 %all_gather.25 = bf16[1536,256]{0,1:T(8,128)(2,1)S(1)} all-gather(bf16[1536,16]{0,1:T(8,128)(2,1)S(1)} %add_convert_fusion.4), channel_id=1, replica_groups=mesh['segment'=4,'chan'=16,'dp'=8] {'chan'}, dimensions={1}, use_global_device_ids=true | all-gather | bytes 835584 | tf_op jit(solution)/shard_map/while/body/eval_jaxpr/all_gather | solution.py:92
  411.2 2.0 multiply_reduce_fusion.15
  426.6 4.6 all-to-all-start.1
  438.6 1.2 copy.289
  441.4 1.5 fusion.364
  442.9 3.9 collective-permute-start
  446.9 1.9 collective-permute-done
  448.9 2.4 copy.95
  451.3 23.8 %all-reduce.18 = (f32[1,2,96]{2,1,0:T(2,128)}, f32[1,2,96]{2,1,0:T(2,128)}) all-reduce(f32[1,2,96]{2,1,0:T(2,128)S(1)} %bitcast.710, f32[1,2,96]{2,1,0:T(2,128)S(1)} %bitcast.711), channel_id=1, replica_groups=mesh['segment'=4,'chan'=16,'dp'=8] {'dp'}, use_global_device_ids=true, to_apply=%region_24.25 | all-reduce | flops 384 | bytes 3072 | tf_op jit(solution)/shard_map/psum | solution.py:171
  475.1 65.7 %all-reduce.22.cloned.1.call-done = (f32[1,2,96,1536]{3,2,1,0:T(8,128)}, f32[1,2,96,432]{3,2,1,0:T(8,128)}) async-done(((f32[1,2,96,1536]{3,2,1,0:T(8,128)}, f32[1,2,96,432]{3,2,1,0:T(8,128)}), (f32[1,2,96,1536]{3,2,1,0:T(8,128)}, f32[1,2,96,432]{3,2,1,0:T(8,128)})) %all-reduce.22.cloned.1.call-update) | async-done | bytes 1511440 | tf_op jit(solution)/shard_map/psum | solution.py:171
  540.8 2.4 copy.359
  (907 shorter events, 182.1 us)
Async XLA Ops:
  7.2 533.6 %all-reduce.22.cloned.1.call-start = ((), (), s32[]{:S(2)}) async-start(), calls=%async_computation.2 | async-start | bytes 3145728 | tf_op jit(solution)/shard_map/psum | solution.py:171
  9.7 29.8 %copy-start.30 = (pred[256]{0:T(512)(128)(4,1)}, pred[256]{0:T(512)(128)(4,1)S(1)}, u32[]{:S(2)}) copy-start(pred[256]{0:T(512)(128)(4,1)S(1)} %compare_and_fusion.7) | copy-start | bytes 772 | tf_op jit(solution)/shard_map/while
  9.7 29.8 %copy-start.27 = (pred[256]{0:T(512)(128)(4,1)}, pred[256]{0:T(512)(128)(4,1)S(1)}, u32[]{:S(2)}) copy-start(pred[256]{0:T(512)(128)(4,1)S(1)} %compare_and_fusion.8) | copy-start | bytes 772 | tf_op jit(solution)/shard_map/while
  39.5 15.8 %copy-start.2 = (bf16[1,1,96,256]{3,2,1,0:T(8,128)(2,1)S(1)}, bf16[1,1,96,256]{3,2,1,0:T(8,128)(2,1)}, u32[]{:S(2)}) copy-start(bf16[1,1,96,256]{3,2,1,0:T(8,128)(2,1)} %get-tuple-element.978) | copy-start | bytes 147460 | tf_op jit(solution)/shard_map/while
  39.8 19.7 %copy-start.7 = (bf16[1,1,96,256]{3,2,1,0:T(8,128)(2,1)S(1)}, bf16[1,1,96,256]{3,2,1,0:T(8,128)(2,1)}, u32[]{:S(2)}) copy-start(bf16[1,1,96,256]{3,2,1,0:T(8,128)(2,1)} %get-tuple-element.981) | copy-start | bytes 147460 | tf_op jit(solution)/shard_map/while
  39.8 19.7 %copy-start.31 = (pred[256]{0:T(512)(128)(4,1)S(1)}, pred[256]{0:T(512)(128)(4,1)}, u32[]{:S(2)}) copy-start(pred[256]{0:T(512)(128)(4,1)} %copy-done.30) | copy-start | bytes 772 | tf_op jit(solution)/shard_map/while
  40.0 20.0 %copy-start.28 = (pred[256]{0:T(512)(128)(4,1)S(1)}, pred[256]{0:T(512)(128)(4,1)}, u32[]{:S(2)}) copy-start(pred[256]{0:T(512)(128)(4,1)} %copy-done.27) | copy-start | bytes 772 | tf_op jit(solution)/shard_map/while
  50.9 12.3 %all-to-all-start = ((bf16[16,96,16]{1,2,0:T(8,128)(2,1)}), bf16[16,96,16]{1,2,0:T(8,128)(2,1)S(1)}, u32[]{:S(2)}, u32[]{:S(2)}) async-start(bf16[16,96,16]{1,2,0:T(8,128)(2,1)} %constant_dynamic-update-slice_fusion.79), calls=%async_computation | async-start | bytes 131072 | tf_op jit(solution)/shard_map/while/body/eval_jaxpr/all_to_all | solution.py:14
  61.9 19.9 %copy-start.22 = (f32[96]{0:T(128)S(1)}, f32[96]{0:T(128)}, u32[]{:S(2)}) copy-start(f32[96]{0:T(128)} %mul.953) | copy-start | bytes 1156 | tf_op jit(solution)/shard_map/while
  85.9 15.9 %copy-start.6 = (bf16[1,1,96,256]{3,2,1,0:T(8,128)(2,1)S(1)}, bf16[1,1,96,256]{3,2,1,0:T(8,128)(2,1)}, u32[]{:S(2)}) copy-start(bf16[1,1,96,256]{3,2,1,0:T(8,128)(2,1)} %get-tuple-element.980) | copy-start | bytes 147460 | tf_op jit(solution)/shard_map/while
  97.2 14.7 %all-to-all-start.1 = ((bf16[16,96,16]{1,2,0:T(8,128)(2,1)}), bf16[16,96,16]{1,2,0:T(8,128)(2,1)S(1)}, u32[]{:S(2)}, u32[]{:S(2)}) async-start(bf16[16,96,16]{1,2,0:T(8,128)(2,1)} %constant_dynamic-update-slice_fusion.95), calls=%async_computation.1 | async-start | bytes 131072 | tf_op jit(solution)/shard_map/while/body/eval_jaxpr/all_to_all | solution.py:14
  111.2 6.3 %copy-start.10 = (f32[2,96]{1,0:T(2,128)S(1)}, f32[2,96]{1,0:T(2,128)}, u32[]{:S(2)}) copy-start(f32[2,96]{1,0:T(2,128)} %get-tuple-element.948) | copy-start | bytes 2308 | tf_op jit(solution)/shard_map/while
  111.2 6.3 %copy-start.13 = (f32[2,96]{1,0:T(2,128)S(1)}, f32[2,96]{1,0:T(2,128)}, u32[]{:S(2)}) copy-start(f32[2,96]{1,0:T(2,128)} %get-tuple-element.949) | copy-start | bytes 2308 | tf_op jit(solution)/shard_map/while
  111.2 6.3 %copy-start.23 = (f32[96]{0:T(128)S(1)}, f32[96]{0:T(128)}, u32[]{:S(2)}) copy-start(f32[96]{0:T(128)} %get-tuple-element.916) | copy-start | bytes 1156 | tf_op jit(solution)/shard_map/while
  111.2 6.3 %copy-start.24 = (f32[96]{0:T(128)S(1)}, f32[96]{0:T(128)}, u32[]{:S(2)}) copy-start(f32[96]{0:T(128)} %get-tuple-element.918) | copy-start | bytes 1156 | tf_op jit(solution)/shard_map/while
  111.2 6.3 %copy-start.25 = (f32[96]{0:T(128)S(1)}, f32[96]{0:T(128)}, u32[]{:S(2)}) copy-start(f32[96]{0:T(128)} %get-tuple-element.917) | copy-start | bytes 1156 | tf_op jit(solution)/shard_map/while
  111.2 6.3 %copy-start.26 = (f32[96]{0:T(128)S(1)}, f32[96]{0:T(128)}, u32[]{:S(2)}) copy-start(f32[96]{0:T(128)} %get-tuple-element.919) | copy-start | bytes 1156 | tf_op jit(solution)/shard_map/while
  111.9 7.6 %copy-start.4 = (f32[2,96,432]{1,2,0:T(8,128)}, f32[2,96,432]{1,2,0:T(8,128)S(1)}, u32[]{:S(2)}) copy-start(f32[2,96,432]{1,2,0:T(8,128)S(1)} %fusion.384) | copy-start | bytes 995332 | tf_op jit(solution)/shard_map/while
  113.5 6.0 %collective-permute-start = (bf16[1536,16]{0,1:T(8,128)(2,1)S(1)}, bf16[1536,16]{0,1:T(8,128)(2,1)S(1)}, u32[]{:S(2)}, u32[]{:S(2)}) collective-permute-start(bf16[1536,16]{0,1:T(8,128)(2,1)S(1)} %get-tuple-element.914), channel_id=1, source_target_pairs={{128,0},{256,128},{384,256},{129,1},{257,129},{385,257},{130,2},{2... | collective-permute-start | bytes 147464 | tf_op jit(solution)/shard_map/while/body/eval_jaxpr/ppermute | solution.py:25
  119.5 29.5 %copy-start.30 = (pred[256]{0:T(512)(128)(4,1)}, pred[256]{0:T(512)(128)(4,1)S(1)}, u32[]{:S(2)}) copy-start(pred[256]{0:T(512)(128)(4,1)S(1)} %compare_and_fusion.7) | copy-start | bytes 772 | tf_op jit(solution)/shard_map/while
  119.6 29.5 %copy-start.27 = (pred[256]{0:T(512)(128)(4,1)}, pred[256]{0:T(512)(128)(4,1)S(1)}, u32[]{:S(2)}) copy-start(pred[256]{0:T(512)(128)(4,1)S(1)} %compare_and_fusion.8) | copy-start | bytes 772 | tf_op jit(solution)/shard_map/while
  149.1 16.0 %copy-start.2 = (bf16[1,1,96,256]{3,2,1,0:T(8,128)(2,1)S(1)}, bf16[1,1,96,256]{3,2,1,0:T(8,128)(2,1)}, u32[]{:S(2)}) copy-start(bf16[1,1,96,256]{3,2,1,0:T(8,128)(2,1)} %get-tuple-element.978) | copy-start | bytes 147460 | tf_op jit(solution)/shard_map/while
  149.4 20.0 %copy-start.7 = (bf16[1,1,96,256]{3,2,1,0:T(8,128)(2,1)S(1)}, bf16[1,1,96,256]{3,2,1,0:T(8,128)(2,1)}, u32[]{:S(2)}) copy-start(bf16[1,1,96,256]{3,2,1,0:T(8,128)(2,1)} %get-tuple-element.981) | copy-start | bytes 147460 | tf_op jit(solution)/shard_map/while
  149.4 20.0 %copy-start.31 = (pred[256]{0:T(512)(128)(4,1)S(1)}, pred[256]{0:T(512)(128)(4,1)}, u32[]{:S(2)}) copy-start(pred[256]{0:T(512)(128)(4,1)} %copy-done.30) | copy-start | bytes 772 | tf_op jit(solution)/shard_map/while
  149.6 20.2 %copy-start.28 = (pred[256]{0:T(512)(128)(4,1)S(1)}, pred[256]{0:T(512)(128)(4,1)}, u32[]{:S(2)}) copy-start(pred[256]{0:T(512)(128)(4,1)} %copy-done.27) | copy-start | bytes 772 | tf_op jit(solution)/shard_map/while
  160.4 12.5 %all-to-all-start = ((bf16[16,96,16]{1,2,0:T(8,128)(2,1)}), bf16[16,96,16]{1,2,0:T(8,128)(2,1)S(1)}, u32[]{:S(2)}, u32[]{:S(2)}) async-start(bf16[16,96,16]{1,2,0:T(8,128)(2,1)} %constant_dynamic-update-slice_fusion.79), calls=%async_computation | async-start | bytes 131072 | tf_op jit(solution)/shard_map/while/body/eval_jaxpr/all_to_all | solution.py:14
  171.7 19.9 %copy-start.22 = (f32[96]{0:T(128)S(1)}, f32[96]{0:T(128)}, u32[]{:S(2)}) copy-start(f32[96]{0:T(128)} %mul.953) | copy-start | bytes 1156 | tf_op jit(solution)/shard_map/while
  195.7 15.9 %copy-start.6 = (bf16[1,1,96,256]{3,2,1,0:T(8,128)(2,1)S(1)}, bf16[1,1,96,256]{3,2,1,0:T(8,128)(2,1)}, u32[]{:S(2)}) copy-start(bf16[1,1,96,256]{3,2,1,0:T(8,128)(2,1)} %get-tuple-element.980) | copy-start | bytes 147460 | tf_op jit(solution)/shard_map/while
  207.0 14.7 %all-to-all-start.1 = ((bf16[16,96,16]{1,2,0:T(8,128)(2,1)}), bf16[16,96,16]{1,2,0:T(8,128)(2,1)S(1)}, u32[]{:S(2)}, u32[]{:S(2)}) async-start(bf16[16,96,16]{1,2,0:T(8,128)(2,1)} %constant_dynamic-update-slice_fusion.95), calls=%async_computation.1 | async-start | bytes 131072 | tf_op jit(solution)/shard_map/while/body/eval_jaxpr/all_to_all | solution.py:14
  221.0 6.3 %copy-start.10 = (f32[2,96]{1,0:T(2,128)S(1)}, f32[2,96]{1,0:T(2,128)}, u32[]{:S(2)}) copy-start(f32[2,96]{1,0:T(2,128)} %get-tuple-element.948) | copy-start | bytes 2308 | tf_op jit(solution)/shard_map/while
  221.0 6.3 %copy-start.13 = (f32[2,96]{1,0:T(2,128)S(1)}, f32[2,96]{1,0:T(2,128)}, u32[]{:S(2)}) copy-start(f32[2,96]{1,0:T(2,128)} %get-tuple-element.949) | copy-start | bytes 2308 | tf_op jit(solution)/shard_map/while
  221.0 6.3 %copy-start.23 = (f32[96]{0:T(128)S(1)}, f32[96]{0:T(128)}, u32[]{:S(2)}) copy-start(f32[96]{0:T(128)} %get-tuple-element.916) | copy-start | bytes 1156 | tf_op jit(solution)/shard_map/while
  221.0 6.3 %copy-start.24 = (f32[96]{0:T(128)S(1)}, f32[96]{0:T(128)}, u32[]{:S(2)}) copy-start(f32[96]{0:T(128)} %get-tuple-element.918) | copy-start | bytes 1156 | tf_op jit(solution)/shard_map/while
  221.0 6.3 %copy-start.25 = (f32[96]{0:T(128)S(1)}, f32[96]{0:T(128)}, u32[]{:S(2)}) copy-start(f32[96]{0:T(128)} %get-tuple-element.917) | copy-start | bytes 1156 | tf_op jit(solution)/shard_map/while
  221.7 7.6 %copy-start.4 = (f32[2,96,432]{1,2,0:T(8,128)}, f32[2,96,432]{1,2,0:T(8,128)S(1)}, u32[]{:S(2)}) copy-start(f32[2,96,432]{1,2,0:T(8,128)S(1)} %fusion.384) | copy-start | bytes 995332 | tf_op jit(solution)/shard_map/while
  223.3 6.0 %collective-permute-start = (bf16[1536,16]{0,1:T(8,128)(2,1)S(1)}, bf16[1536,16]{0,1:T(8,128)(2,1)S(1)}, u32[]{:S(2)}, u32[]{:S(2)}) collective-permute-start(bf16[1536,16]{0,1:T(8,128)(2,1)S(1)} %get-tuple-element.914), channel_id=1, source_target_pairs={{128,0},{256,128},{384,256},{129,1},{257,129},{385,257},{130,2},{2... | collective-permute-start | bytes 147464 | tf_op jit(solution)/shard_map/while/body/eval_jaxpr/ppermute | solution.py:25
  229.3 29.5 %copy-start.30 = (pred[256]{0:T(512)(128)(4,1)}, pred[256]{0:T(512)(128)(4,1)S(1)}, u32[]{:S(2)}) copy-start(pred[256]{0:T(512)(128)(4,1)S(1)} %compare_and_fusion.7) | copy-start | bytes 772 | tf_op jit(solution)/shard_map/while
  229.4 29.5 %copy-start.27 = (pred[256]{0:T(512)(128)(4,1)}, pred[256]{0:T(512)(128)(4,1)S(1)}, u32[]{:S(2)}) copy-start(pred[256]{0:T(512)(128)(4,1)S(1)} %compare_and_fusion.8) | copy-start | bytes 772 | tf_op jit(solution)/shard_map/while
  258.9 16.0 %copy-start.2 = (bf16[1,1,96,256]{3,2,1,0:T(8,128)(2,1)S(1)}, bf16[1,1,96,256]{3,2,1,0:T(8,128)(2,1)}, u32[]{:S(2)}) copy-start(bf16[1,1,96,256]{3,2,1,0:T(8,128)(2,1)} %get-tuple-element.978) | copy-start | bytes 147460 | tf_op jit(solution)/shard_map/while
  259.2 20.0 %copy-start.7 = (bf16[1,1,96,256]{3,2,1,0:T(8,128)(2,1)S(1)}, bf16[1,1,96,256]{3,2,1,0:T(8,128)(2,1)}, u32[]{:S(2)}) copy-start(bf16[1,1,96,256]{3,2,1,0:T(8,128)(2,1)} %get-tuple-element.981) | copy-start | bytes 147460 | tf_op jit(solution)/shard_map/while
  259.2 20.0 %copy-start.31 = (pred[256]{0:T(512)(128)(4,1)S(1)}, pred[256]{0:T(512)(128)(4,1)}, u32[]{:S(2)}) copy-start(pred[256]{0:T(512)(128)(4,1)} %copy-done.30) | copy-start | bytes 772 | tf_op jit(solution)/shard_map/while
  259.4 20.2 %copy-start.28 = (pred[256]{0:T(512)(128)(4,1)S(1)}, pred[256]{0:T(512)(128)(4,1)}, u32[]{:S(2)}) copy-start(pred[256]{0:T(512)(128)(4,1)} %copy-done.27) | copy-start | bytes 772 | tf_op jit(solution)/shard_map/while
  270.2 12.5 %all-to-all-start = ((bf16[16,96,16]{1,2,0:T(8,128)(2,1)}), bf16[16,96,16]{1,2,0:T(8,128)(2,1)S(1)}, u32[]{:S(2)}, u32[]{:S(2)}) async-start(bf16[16,96,16]{1,2,0:T(8,128)(2,1)} %constant_dynamic-update-slice_fusion.79), calls=%async_computation | async-start | bytes 131072 | tf_op jit(solution)/shard_map/while/body/eval_jaxpr/all_to_all | solution.py:14
  281.5 19.9 %copy-start.22 = (f32[96]{0:T(128)S(1)}, f32[96]{0:T(128)}, u32[]{:S(2)}) copy-start(f32[96]{0:T(128)} %mul.953) | copy-start | bytes 1156 | tf_op jit(solution)/shard_map/while
  305.5 15.9 %copy-start.6 = (bf16[1,1,96,256]{3,2,1,0:T(8,128)(2,1)S(1)}, bf16[1,1,96,256]{3,2,1,0:T(8,128)(2,1)}, u32[]{:S(2)}) copy-start(bf16[1,1,96,256]{3,2,1,0:T(8,128)(2,1)} %get-tuple-element.980) | copy-start | bytes 147460 | tf_op jit(solution)/shard_map/while
  316.8 14.7 %all-to-all-start.1 = ((bf16[16,96,16]{1,2,0:T(8,128)(2,1)}), bf16[16,96,16]{1,2,0:T(8,128)(2,1)S(1)}, u32[]{:S(2)}, u32[]{:S(2)}) async-start(bf16[16,96,16]{1,2,0:T(8,128)(2,1)} %constant_dynamic-update-slice_fusion.95), calls=%async_computation.1 | async-start | bytes 131072 | tf_op jit(solution)/shard_map/while/body/eval_jaxpr/all_to_all | solution.py:14
  330.8 6.3 %copy-start.10 = (f32[2,96]{1,0:T(2,128)S(1)}, f32[2,96]{1,0:T(2,128)}, u32[]{:S(2)}) copy-start(f32[2,96]{1,0:T(2,128)} %get-tuple-element.948) | copy-start | bytes 2308 | tf_op jit(solution)/shard_map/while
  330.8 6.3 %copy-start.13 = (f32[2,96]{1,0:T(2,128)S(1)}, f32[2,96]{1,0:T(2,128)}, u32[]{:S(2)}) copy-start(f32[2,96]{1,0:T(2,128)} %get-tuple-element.949) | copy-start | bytes 2308 | tf_op jit(solution)/shard_map/while
  331.5 7.6 %copy-start.4 = (f32[2,96,432]{1,2,0:T(8,128)}, f32[2,96,432]{1,2,0:T(8,128)S(1)}, u32[]{:S(2)}) copy-start(f32[2,96,432]{1,2,0:T(8,128)S(1)} %fusion.384) | copy-start | bytes 995332 | tf_op jit(solution)/shard_map/while
  333.1 6.0 %collective-permute-start = (bf16[1536,16]{0,1:T(8,128)(2,1)S(1)}, bf16[1536,16]{0,1:T(8,128)(2,1)S(1)}, u32[]{:S(2)}, u32[]{:S(2)}) collective-permute-start(bf16[1536,16]{0,1:T(8,128)(2,1)S(1)} %get-tuple-element.914), channel_id=1, source_target_pairs={{128,0},{256,128},{384,256},{129,1},{257,129},{385,257},{130,2},{2... | collective-permute-start | bytes 147464 | tf_op jit(solution)/shard_map/while/body/eval_jaxpr/ppermute | solution.py:25
  339.1 29.5 %copy-start.30 = (pred[256]{0:T(512)(128)(4,1)}, pred[256]{0:T(512)(128)(4,1)S(1)}, u32[]{:S(2)}) copy-start(pred[256]{0:T(512)(128)(4,1)S(1)} %compare_and_fusion.7) | copy-start | bytes 772 | tf_op jit(solution)/shard_map/while
  339.1 29.5 %copy-start.27 = (pred[256]{0:T(512)(128)(4,1)}, pred[256]{0:T(512)(128)(4,1)S(1)}, u32[]{:S(2)}) copy-start(pred[256]{0:T(512)(128)(4,1)S(1)} %compare_and_fusion.8) | copy-start | bytes 772 | tf_op jit(solution)/shard_map/while
  368.6 16.0 %copy-start.2 = (bf16[1,1,96,256]{3,2,1,0:T(8,128)(2,1)S(1)}, bf16[1,1,96,256]{3,2,1,0:T(8,128)(2,1)}, u32[]{:S(2)}) copy-start(bf16[1,1,96,256]{3,2,1,0:T(8,128)(2,1)} %get-tuple-element.978) | copy-start | bytes 147460 | tf_op jit(solution)/shard_map/while
  368.9 20.0 %copy-start.7 = (bf16[1,1,96,256]{3,2,1,0:T(8,128)(2,1)S(1)}, bf16[1,1,96,256]{3,2,1,0:T(8,128)(2,1)}, u32[]{:S(2)}) copy-start(bf16[1,1,96,256]{3,2,1,0:T(8,128)(2,1)} %get-tuple-element.981) | copy-start | bytes 147460 | tf_op jit(solution)/shard_map/while
  369.0 20.0 %copy-start.31 = (pred[256]{0:T(512)(128)(4,1)S(1)}, pred[256]{0:T(512)(128)(4,1)}, u32[]{:S(2)}) copy-start(pred[256]{0:T(512)(128)(4,1)} %copy-done.30) | copy-start | bytes 772 | tf_op jit(solution)/shard_map/while
  369.1 20.2 %copy-start.28 = (pred[256]{0:T(512)(128)(4,1)S(1)}, pred[256]{0:T(512)(128)(4,1)}, u32[]{:S(2)}) copy-start(pred[256]{0:T(512)(128)(4,1)} %copy-done.27) | copy-start | bytes 772 | tf_op jit(solution)/shard_map/while
  380.0 12.5 %all-to-all-start = ((bf16[16,96,16]{1,2,0:T(8,128)(2,1)}), bf16[16,96,16]{1,2,0:T(8,128)(2,1)S(1)}, u32[]{:S(2)}, u32[]{:S(2)}) async-start(bf16[16,96,16]{1,2,0:T(8,128)(2,1)} %constant_dynamic-update-slice_fusion.79), calls=%async_computation | async-start | bytes 131072 | tf_op jit(solution)/shard_map/while/body/eval_jaxpr/all_to_all | solution.py:14
  391.3 19.9 %copy-start.22 = (f32[96]{0:T(128)S(1)}, f32[96]{0:T(128)}, u32[]{:S(2)}) copy-start(f32[96]{0:T(128)} %mul.953) | copy-start | bytes 1156 | tf_op jit(solution)/shard_map/while
  415.3 15.9 %copy-start.6 = (bf16[1,1,96,256]{3,2,1,0:T(8,128)(2,1)S(1)}, bf16[1,1,96,256]{3,2,1,0:T(8,128)(2,1)}, u32[]{:S(2)}) copy-start(bf16[1,1,96,256]{3,2,1,0:T(8,128)(2,1)} %get-tuple-element.980) | copy-start | bytes 147460 | tf_op jit(solution)/shard_map/while
  426.6 14.7 %all-to-all-start.1 = ((bf16[16,96,16]{1,2,0:T(8,128)(2,1)}), bf16[16,96,16]{1,2,0:T(8,128)(2,1)S(1)}, u32[]{:S(2)}, u32[]{:S(2)}) async-start(bf16[16,96,16]{1,2,0:T(8,128)(2,1)} %constant_dynamic-update-slice_fusion.95), calls=%async_computation.1 | async-start | bytes 131072 | tf_op jit(solution)/shard_map/while/body/eval_jaxpr/all_to_all | solution.py:14
  440.5 6.3 %copy-start.10 = (f32[2,96]{1,0:T(2,128)S(1)}, f32[2,96]{1,0:T(2,128)}, u32[]{:S(2)}) copy-start(f32[2,96]{1,0:T(2,128)} %get-tuple-element.948) | copy-start | bytes 2308 | tf_op jit(solution)/shard_map/while
  440.6 6.3 %copy-start.13 = (f32[2,96]{1,0:T(2,128)S(1)}, f32[2,96]{1,0:T(2,128)}, u32[]{:S(2)}) copy-start(f32[2,96]{1,0:T(2,128)} %get-tuple-element.949) | copy-start | bytes 2308 | tf_op jit(solution)/shard_map/while
  441.3 7.6 %copy-start.4 = (f32[2,96,432]{1,2,0:T(8,128)}, f32[2,96,432]{1,2,0:T(8,128)S(1)}, u32[]{:S(2)}) copy-start(f32[2,96,432]{1,2,0:T(8,128)S(1)} %fusion.384) | copy-start | bytes 995332 | tf_op jit(solution)/shard_map/while
  442.9 6.0 %collective-permute-start = (bf16[1536,16]{0,1:T(8,128)(2,1)S(1)}, bf16[1536,16]{0,1:T(8,128)(2,1)S(1)}, u32[]{:S(2)}, u32[]{:S(2)}) collective-permute-start(bf16[1536,16]{0,1:T(8,128)(2,1)S(1)} %get-tuple-element.914), channel_id=1, source_target_pairs={{128,0},{256,128},{384,256},{129,1},{257,129},{385,257},{130,2},{2... | collective-permute-start | bytes 147464 | tf_op jit(solution)/shard_map/while/body/eval_jaxpr/ppermute | solution.py:25
  (69 other events, 164.5 us)
Sparse Core Ops, SparseCore 0:
  451.4 89.3 all-reduce.21
